TPU v7x, 32 devices: a whole 2x2x4 slice. The times are simulated.
32 devices in a mesh: section: 2 (over y), fsdp: 4 (over x, core), replica: 4 (over z).
Axes of the slice: x: 2, y: 2, z: 4, core: 2. Of those that a mesh axis runs over, the one named last changes fastest.
Arguments:
- images: bfloat16 [4, 32, 14, 14, 512], P(None, ('fsdp', 'replica')), may hold values from -6 to 6
- cotangent: bfloat16 [4, 32, 14, 14, 512], P(None, ('fsdp', 'replica')), may hold values from -6 to 6
- counts: int32 [4, 16], P(None, ('fsdp', 'replica')), may hold values from 1 to 2, as said below
- regions: int32 [14, 14], replicated, may hold values from 0 to 8, as said below
- relpos: int32 [49, 49], replicated, may hold values from 0 to 168, as said below
- qkv_weight: bfloat16 [2, 512, 1536], P('section', 'fsdp'), may hold values from -0.25 to 0.25
- proj_weight: bfloat16 [2, 512, 512], P('section', 'fsdp'), may hold values from -1.5 to 1.5
- fc1_weight: bfloat16 [2, 512, 2048], P('section', 'fsdp'), may hold values from -0.25 to 0.25
- fc2_weight: bfloat16 [2, 2048, 512], P('section', 'fsdp'), may hold values from -0.125 to 0.125
- gains: bfloat16 [2, 2, 512], P('section', None, 'fsdp'), may hold values from 0.099609375 to 1.8984375
- biases: bfloat16 [2, 6, 512], P('section', None, 'fsdp'), may hold values from -3 to 3
- fc1_bias: bfloat16 [2, 2048], P('section', 'fsdp'), may hold values from -3 to 3
- rel_table: bfloat16 [2, 169, 16], P('section', None, 'fsdp'), may hold values from -5 to 5
Outputs:
- block_out: bfloat16 [2, 4, 32, 14, 14, 512], P('section', None, ('fsdp', 'replica'))
- input_grad: float32 [2, 4, 32, 14, 14, 512], P('section', None, ('fsdp', 'replica'))
- grad_qkv: float32 [2, 512, 1536], P('section', 'fsdp')
- grad_proj: float32 [2, 512, 512], P('section', 'fsdp')
- grad_fc1: float32 [2, 512, 2048], P('section', 'fsdp')
- grad_fc2: float32 [2, 2048, 512], P('section', 'fsdp')
- grad_gains: float32 [2, 2, 512], P('section', None, 'fsdp')
- grad_biases: float32 [2, 6, 512], P('section', None, 'fsdp')
- grad_fc1_bias: float32 [2, 2048], P('section', 'fsdp')
- grad_table: float32 [2, 169, 16], P('section', None, 'fsdp')
Inputs may be any that keep to these rules, and one draw needn't show every extreme that they name: `counts`: slots 0 to count - 1 of a device's 2 slots in a micro-batch are live; in every micro-batch some device has all 2 live. `regions`: region ids are constant on bands: id = 3 * band(row) + band(column) with the same two cut positions for rows and columns. `relpos`: pairs with the same relative offset share a row; every row is used.
All inputs are finite; a program needn't handle non-finite values.
Results may differ from a plain program's by a relative error of at most 0.019.
Values may be sent and summed in bfloat16 or wider, within the bound.
No kernel may reach another device: no remote copies, remote signals or barrier semaphores. Data moves between devices by JAX's collectives and lax.ppermute only.
A program may use at most 320 MiB of HBM per device.

v0:
```python
import jax
import jax.numpy as jnp
from jax import lax
from jax.sharding import PartitionSpec as P

DIM = 512
HEADS = 16
HEAD_DIM = 32
WIN = 7
SIDE = 14
SHIFT = 3
TABLE = 169
EPSILON = 1e-05
ROOT_HALF = 0.7071067811865476
INV_ROOT_TAU = 0.3989422804014327


def shifted(value, axis, by):
    length = lax.axis_size(axis)
    pairs = [(i, i + by) for i in range(length) if 0 <= i + by < length]
    return lax.ppermute(value, axis, pairs)


def layer_norm(values, gain, offset_row):
    center = values - jnp.mean(values, axis=-1, keepdims=True)
    spread = jnp.mean(center * center, axis=-1, keepdims=True)
    scaled = lax.rsqrt(spread + EPSILON)
    normed = center * scaled
    return (normed * gain + offset_row, normed, scaled)


def norm_backward(upstream, normed, scaled, gain):
    direct = upstream * gain
    return (
        direct
        - jnp.mean(direct, axis=-1, keepdims=True)
        - normed * jnp.mean(direct * normed, axis=-1, keepdims=True)
    ) * scaled


def gelu_value(before):
    return 0.5 * before * (1.0 + jax.scipy.special.erf(before * ROOT_HALF))


def gelu_slope(before):
    return 0.5 * (
        1.0 + jax.scipy.special.erf(before * ROOT_HALF)
    ) + before * INV_ROOT_TAU * jnp.exp(-0.5 * before * before)


def inner_rows(left, right):
    return lax.dot_general(
        left, right, (((0,), (0,)), ((), ())), preferred_element_type=jnp.float32
    )


def outer_cols(left, right):
    return lax.dot_general(
        left, right, (((1,), (1,)), ((), ())), preferred_element_type=jnp.float32
    )


def to_windows(image_rows, offset):
    rolled = jnp.roll(image_rows, (-offset, -offset), axis=(1, 2))
    count = image_rows.shape[0]
    parts = SIDE // WIN
    shaped = rolled.reshape(count, parts, WIN, parts, WIN, DIM).transpose(0, 1, 3, 2, 4, 5)
    return shaped.reshape(count * SIDE * SIDE, DIM)


def from_windows(window_rows, offset):
    count = window_rows.shape[0] // (SIDE * SIDE)
    parts = SIDE // WIN
    shaped = window_rows.reshape(count, parts, parts, WIN, WIN, DIM).transpose(0, 1, 3, 2, 4, 5)
    return jnp.roll(shaped.reshape(count, SIDE, SIDE, DIM), (offset, offset), axis=(1, 2))


def relation_onehot(relpos):
    flat = relpos.reshape(-1)
    return (flat[:, None] == jnp.arange(TABLE, dtype=jnp.int32)[None, :]).astype(jnp.float32)


def region_mask(regions, later):
    parts = SIDE // WIN
    tiles = (
        regions.reshape(parts, WIN, parts, WIN)
        .transpose(0, 2, 1, 3)
        .reshape(parts * parts, WIN * WIN)
    )
    differ = (tiles[:, :, None] != tiles[:, None, :]) & later
    return jnp.where(differ, jnp.float32(-100.0), jnp.float32(0.0))


def window_eye():
    count = (SIDE // WIN) ** 2
    return lax.broadcasted_iota(jnp.int32, (count, count), 0) == lax.broadcasted_iota(
        jnp.int32, (count, count), 1
    )


def attention_add(table, onehot, masking):
    lookup = jnp.dot(onehot, table.astype(jnp.float32), precision=lax.Precision.HIGHEST)
    lookup = lookup.reshape(WIN * WIN, WIN * WIN, HEADS).transpose(2, 0, 1)
    windowed = lookup[None] + masking[:, None]
    count = (SIDE // WIN) ** 2
    eye = window_eye()
    spread_add = jnp.where(
        eye[None, :, None, :, None],
        windowed.transpose(1, 0, 2, 3)[:, :, :, None, :],
        jnp.float32(0.0),
    )
    full_add = spread_add.reshape(HEADS, count * WIN * WIN, count * WIN * WIN)
    same = jnp.broadcast_to(eye[:, None, :, None], (count, WIN * WIN, count, WIN * WIN)).reshape(
        count * WIN * WIN, count * WIN * WIN
    )
    return (full_add, same)


def forward(rows, params, added):
    qkv_w, proj_w, fc1_w, fc2_w, gain_rows, bias_rows, fc1_b, table = params
    full_add, same = added
    gains_f = gain_rows.astype(jnp.float32)
    biases_f = bias_rows.astype(jnp.float32)
    factor = HEAD_DIM ** (-0.5)
    base = rows.astype(jnp.float32)
    first, normed_a, scaled_a = layer_norm(base, gains_f[0], biases_f[0])
    first_b = first.astype(jnp.bfloat16)
    mixed = jnp.dot(first_b, qkv_w, preferred_element_type=jnp.float32)
    count = rows.shape[0] // (SIDE * SIDE)
    blocks = (count, SIDE * SIDE, HEADS, HEAD_DIM)
    query_blocks = ((mixed[:, :DIM] + biases_f[1]) * factor).astype(jnp.bfloat16).reshape(blocks)
    key_blocks = mixed[:, DIM : 2 * DIM].astype(jnp.bfloat16).reshape(blocks)
    value_blocks = (mixed[:, 2 * DIM :] + biases_f[2]).astype(jnp.bfloat16).reshape(blocks)
    scores = (
        jnp.einsum("sihd,sjhd->shij", query_blocks, key_blocks, preferred_element_type=jnp.float32)
        + full_add[None]
    )
    expo = jnp.where(same[None, None], jnp.exp(scores), jnp.float32(0.0))
    probs = expo / jnp.sum(expo, axis=-1, keepdims=True)
    probs_b = probs.astype(jnp.bfloat16)
    attended = jnp.einsum(
        "shij,sjhd->sihd", probs_b, value_blocks, preferred_element_type=jnp.float32
    )
    attended = attended.astype(jnp.bfloat16).reshape(rows.shape[0], DIM)
    middle = base + jnp.dot(attended, proj_w, preferred_element_type=jnp.float32) + biases_f[3]
    second, normed_b, scaled_b = layer_norm(middle, gains_f[1], biases_f[4])
    second_b = second.astype(jnp.bfloat16)
    before = jnp.dot(second_b, fc1_w, preferred_element_type=jnp.float32) + fc1_b.astype(
        jnp.float32
    )
    hidden_b = gelu_value(before).astype(jnp.bfloat16)
    output = middle + jnp.dot(hidden_b, fc2_w, preferred_element_type=jnp.float32) + biases_f[5]
    saved = (
        normed_a,
        scaled_a,
        first_b,
        query_blocks,
        key_blocks,
        value_blocks,
        probs,
        probs_b,
        attended,
        normed_b,
        scaled_b,
        second_b,
        before,
        hidden_b,
    )
    return (output.astype(jnp.bfloat16), saved)


def backward(upstream_rows, saved, params, onehot):
    qkv_w, proj_w, fc1_w, fc2_w, gain_rows, bias_rows, fc1_b, table = params
    gains_f = gain_rows.astype(jnp.float32)
    factor = HEAD_DIM ** (-0.5)
    (
        normed_a,
        scaled_a,
        first_b,
        query_blocks,
        key_blocks,
        value_blocks,
        probs,
        probs_b,
        attended,
        normed_b,
        scaled_b,
        second_b,
        before,
        hidden_b,
    ) = saved
    upstream = upstream_rows.astype(jnp.float32)
    grad_fc2_bias = jnp.sum(upstream, axis=0)
    grad_fc2 = inner_rows(hidden_b, upstream_rows)
    grad_before = outer_cols(upstream_rows, fc2_w) * gelu_slope(before)
    grad_before_b = grad_before.astype(jnp.bfloat16)
    grad_fc1_bias = jnp.sum(grad_before, axis=0)
    grad_fc1 = inner_rows(second_b, grad_before_b)
    grad_second = outer_cols(grad_before_b, fc1_w)
    grad_gain_b = jnp.sum(grad_second * normed_b, axis=0)
    grad_shift_b = jnp.sum(grad_second, axis=0)
    grad_middle = upstream + norm_backward(grad_second, normed_b, scaled_b, gains_f[1])
    grad_middle_b = grad_middle.astype(jnp.bfloat16)
    grad_proj_bias = jnp.sum(grad_middle, axis=0)
    grad_proj = inner_rows(attended, grad_middle_b)
    grad_attended = (
        outer_cols(grad_middle_b, proj_w).astype(jnp.bfloat16).reshape(query_blocks.shape)
    )
    grad_probs = jnp.einsum(
        "sihd,sjhd->shij", grad_attended, value_blocks, preferred_element_type=jnp.float32
    )
    grad_scores = probs * (grad_probs - jnp.sum(probs * grad_probs, axis=-1, keepdims=True))
    grad_scores_b = grad_scores.astype(jnp.bfloat16)
    count = (SIDE // WIN) ** 2
    summed = jnp.sum(grad_scores, axis=0).reshape(HEADS, count, WIN * WIN, count, WIN * WIN)
    eye_f = window_eye().astype(jnp.float32)
    table_terms = jnp.einsum(
        "hwivj,wv->ijh", summed, eye_f, precision=lax.Precision.HIGHEST
    ).reshape(WIN**4, HEADS)
    grad_table = lax.dot_general(
        onehot, table_terms, (((0,), (0,)), ((), ())), precision=lax.Precision.HIGHEST
    )
    total_rows = first_b.shape[0]
    grad_queries = (
        jnp.einsum("shij,sjhd->sihd", grad_scores_b, key_blocks, preferred_element_type=jnp.float32)
        * factor
    ).reshape(total_rows, DIM)
    grad_keys = jnp.einsum(
        "shij,sihd->sjhd", grad_scores_b, query_blocks, preferred_element_type=jnp.float32
    ).reshape(total_rows, DIM)
    grad_values = jnp.einsum(
        "shij,sihd->sjhd", probs_b, grad_attended, preferred_element_type=jnp.float32
    ).reshape(total_rows, DIM)
    grad_mixed_b = jnp.concatenate([grad_queries, grad_keys, grad_values], axis=1).astype(
        jnp.bfloat16
    )
    grad_qkv = inner_rows(first_b, grad_mixed_b)
    grad_first = outer_cols(grad_mixed_b, qkv_w)
    grad_gain_a = jnp.sum(grad_first * normed_a, axis=0)
    grad_shift_a = jnp.sum(grad_first, axis=0)
    grad_rows = grad_middle + norm_backward(grad_first, normed_a, scaled_a, gains_f[0])
    grad_gains = jnp.stack([grad_gain_a, grad_gain_b])
    grad_biases = jnp.stack(
        [
            grad_shift_a,
            jnp.sum(grad_queries, axis=0),
            jnp.sum(grad_values, axis=0),
            grad_proj_bias,
            grad_shift_b,
            grad_fc2_bias,
        ]
    )
    return (
        grad_rows,
        (
            grad_qkv,
            grad_proj,
            grad_fc1,
            grad_fc2,
            grad_gains,
            grad_biases,
            grad_fc1_bias,
            grad_table,
        ),
    )


def keep_slot(store, fresh, place, valid):
    former = lax.dynamic_index_in_dim(store, place, 0, keepdims=False)
    return lax.dynamic_update_index_in_dim(store, jnp.where(valid, fresh, former), place, 0)


def add_trees(left, right):
    if left is None:
        return right
    return jax.tree.map(lambda first, second: first + second, left, right)


def shards(
    images,
    cotangent,
    counts,
    regions,
    relpos,
    qkv_weight,
    proj_weight,
    fc1_weight,
    fc2_weight,
    gains,
    biases,
    fc1_bias,
    rel_table,
):
    section = lax.axis_index("section")
    later = section == 1
    offset = SHIFT * section
    micro = images.shape[0]
    slots = images.shape[1]
    live = lax.broadcasted_iota(jnp.int32, (micro, slots), 1) < counts
    onehot = relation_onehot(relpos)
    masking = region_mask(regions, later)
    zero_half = jnp.zeros((), jnp.bfloat16)
    held = (
        lax.all_gather(qkv_weight[0], "fsdp", axis=0, tiled=True),
        lax.all_gather(proj_weight[0], "fsdp", axis=0, tiled=True),
        lax.all_gather(fc1_weight[0], "fsdp", axis=0, tiled=True),
        lax.all_gather(fc2_weight[0], "fsdp", axis=0, tiled=True),
        lax.all_gather(gains[0], "fsdp", axis=1, tiled=True),
        lax.all_gather(biases[0], "fsdp", axis=1, tiled=True),
        lax.all_gather(fc1_bias[0], "fsdp", axis=0, tiled=True),
        lax.all_gather(rel_table[0], "fsdp", axis=1, tiled=True),
    )

    def fetch():
        return held

    carried = jnp.zeros(images.shape[1:], jnp.bfloat16)
    inputs_kept = jnp.zeros_like(images)
    outputs = jnp.zeros_like(images)
    for moment in range(micro + 1):
        position = moment - section
        valid = (position >= 0) & (position < micro)
        place = jnp.clip(position, 0, micro - 1)
        source = jnp.where(later, carried, images[min(moment, micro - 1)])
        params = fetch()
        added = attention_add(params[7], onehot, masking)
        result_rows, unused = forward(to_windows(source, offset), params, added)
        alive = lax.dynamic_index_in_dim(live, place, 0, keepdims=False)[:, None, None, None]
        result = jnp.where(alive, from_windows(result_rows, offset), zero_half)
        inputs_kept = keep_slot(inputs_kept, source, place, valid)
        outputs = keep_slot(outputs, result, place, valid)
        if moment < micro:
            carried = shifted(result, "section", 1)
    returned = jnp.zeros(images.shape[1:], jnp.bfloat16)
    input_grads = jnp.zeros(images.shape, jnp.float32)
    totals = None
    for moment in range(micro + 1):
        position = moment - 1 + section
        valid = (position >= 0) & (position < micro)
        place = jnp.clip(position, 0, micro - 1)
        alive = lax.dynamic_index_in_dim(live, place, 0, keepdims=False)[:, None, None, None]
        incoming = jnp.where(later, cotangent[min(moment, micro - 1)], returned)
        incoming = jnp.where(valid & alive, incoming, zero_half)
        source = lax.dynamic_index_in_dim(inputs_kept, place, 0, keepdims=False)
        params = fetch()
        added = attention_add(params[7], onehot, masking)
        unused, saved = forward(to_windows(source, offset), params, added)
        grad_rows, terms = backward(to_windows(incoming, offset), saved, params, onehot)
        grad_input = from_windows(grad_rows, offset)
        input_grads = keep_slot(input_grads, grad_input, place, valid)
        totals = add_trees(totals, terms)
        if moment < micro:
            returned = shifted(grad_input.astype(jnp.bfloat16), "section", -1)
    parted = (
        lax.psum_scatter(
            totals[0].astype(jnp.bfloat16), "fsdp", scatter_dimension=0, tiled=True
        ).astype(jnp.float32),
        lax.psum_scatter(
            totals[1].astype(jnp.bfloat16), "fsdp", scatter_dimension=0, tiled=True
        ).astype(jnp.float32),
        lax.psum_scatter(
            totals[2].astype(jnp.bfloat16), "fsdp", scatter_dimension=0, tiled=True
        ).astype(jnp.float32),
        lax.psum_scatter(
            totals[3].astype(jnp.bfloat16), "fsdp", scatter_dimension=0, tiled=True
        ).astype(jnp.float32),
        lax.psum_scatter(
            totals[4].astype(jnp.bfloat16), "fsdp", scatter_dimension=1, tiled=True
        ).astype(jnp.float32),
        lax.psum_scatter(
            totals[5].astype(jnp.bfloat16), "fsdp", scatter_dimension=1, tiled=True
        ).astype(jnp.float32),
        lax.psum_scatter(
            totals[6].astype(jnp.bfloat16), "fsdp", scatter_dimension=0, tiled=True
        ).astype(jnp.float32),
        lax.psum_scatter(
            totals[7].astype(jnp.bfloat16), "fsdp", scatter_dimension=1, tiled=True
        ).astype(jnp.float32),
    )
    shares = (
        lax.psum(parted[0].astype(jnp.bfloat16), "replica").astype(jnp.float32),
        lax.psum(parted[1].astype(jnp.bfloat16), "replica").astype(jnp.float32),
        lax.psum(parted[2].astype(jnp.bfloat16), "replica").astype(jnp.float32),
        lax.psum(parted[3].astype(jnp.bfloat16), "replica").astype(jnp.float32),
        lax.psum(parted[4].astype(jnp.bfloat16), "replica").astype(jnp.float32),
        lax.psum(parted[5].astype(jnp.bfloat16), "replica").astype(jnp.float32),
        lax.psum(parted[6].astype(jnp.bfloat16), "replica").astype(jnp.float32),
        lax.psum(parted[7].astype(jnp.bfloat16), "replica").astype(jnp.float32),
    )
    return (
        outputs[None],
        input_grads[None],
        shares[0][None],
        shares[1][None],
        shares[2][None],
        shares[3][None],
        shares[4][None],
        shares[5][None],
        shares[6][None],
        shares[7][None],
    )


def solution(mesh):
    in_specs = (
        P(None, ("fsdp", "replica"), None, None, None),
        P(None, ("fsdp", "replica"), None, None, None),
        P(None, ("fsdp", "replica")),
        P(),
        P(),
        P("section", "fsdp", None),
        P("section", "fsdp", None),
        P("section", "fsdp", None),
        P("section", "fsdp", None),
        P("section", None, "fsdp"),
        P("section", None, "fsdp"),
        P("section", "fsdp"),
        P("section", None, "fsdp"),
    )
    out_specs = (
        P("section", None, ("fsdp", "replica"), None, None, None),
        P("section", None, ("fsdp", "replica"), None, None, None),
        P("section", "fsdp", None),
        P("section", "fsdp", None),
        P("section", "fsdp", None),
        P("section", "fsdp", None),
        P("section", None, "fsdp"),
        P("section", None, "fsdp"),
        P("section", "fsdp"),
        P("section", None, "fsdp"),
    )
    return jax.shard_map(shards, mesh=mesh, in_specs=in_specs, out_specs=out_specs, check_vma=False)
```

profile of v0, /device:TPU:0, one launch (start us, length us, event | category | flops | bytes accessed | tf_op | source)
XLA Modules:
  0.0 1292.6 jit_solution(11657054412358554816)
XLA Ops:
  9.5 6.3 all-gather.1
  48.0 10.8 all-gather.4
  116.6 11.8 fusion.474
  178.5 5.9 fusion.235
  520.8 16.6 %fusion.14 = (f32[2,16,196]{2,1,0:T(8,128)S(1)}, f32[2,16,196]{2,1,0:T(8,128)}, f32[2,16,196]{2,1,0:T(8,128)S(1)}, f32[2,16,196]{2,1,0:T(8,128)S(1)}, f32[2,16,1...) fusion(f32[16,196,196]{1,2,0:T(8,128)S(1)} %copy.870, ...), kind=kOutput, calls=%fused_computation.39 | convolution fusion | flops 100765952 | bytes 32953872 | tf_op jit(solution)/shard_map/sihd,sjhd->shij/dot_general | solution.py:135
  537.4 19.7 %fusion.13 = (f32[2,16,196,196]{2,3,1,0:T(8,128)}, f32[2,16,196,196]{2,3,1,0:T(8,128)S(1)}, f32[2,16,196,196]{2,3,1,0:T(8,128)}, f32[2,16,196,196]{2,3,1,0:T(8,128)}, f32[2,16,196,196]{2,3,1,0:T(8,128)}) fusion(f32[2,16,196,196]{2,3,1,0:T(8,128)} %get-tuple-element.238, f32[2,16,196]{2,1,0:T(8,128)S(1)} %get-tuple-element.42, f32[16,196,196]{1,2,0:T(8,128)S(1)} %copy.870, ...), kind=kLoop, calls=%fused_computation.38 | loop fusion | flops 18439680 | bytes 51794960 | tf_op jit(solution)/shard_map/div | solution.py:139
  584.3 7.0 multiply_reduce_fusion.4
  591.2 8.1 fusion.41
  745.0 7.0 multiply_reduce_fusion.3
  752.0 7.6 fusion.43
  812.5 7.0 multiply_reduce_fusion.2
  819.5 7.6 fusion.45
  878.2 7.0 multiply_reduce_fusion.1
  885.2 7.6 fusion.47
  943.1 7.0 multiply_reduce_fusion
  950.1 7.7 fusion.49
  1012.1 12.7 copy.1077
  1024.9 8.1 fusion.661
  1044.1 6.5 reshape.1264
  1050.5 13.1 %copy.1079 = f32[16,4,49,4,49]{4,3,1,2,0:T(4,128)} copy(f32[16,4,49,4,49]{2,1,4,3,0:T(4,128)} %reshape.1264) | data formatting | bytes 4917248 | tf_op jit(solution)/shard_map/reshape | solution.py:215
  1075.0 8.0 fusion.662
  1091.2 6.7 reshape.1265
  1097.9 12.7 copy.1081
  1110.7 8.0 fusion.663
  1129.1 6.5 reshape.1266
  1135.6 12.9 copy.1083
  1148.6 8.1 fusion.664
  1177.8 12.7 copy.1085
  1190.6 8.2 fusion.665
  1200.9 10.1 all-reduce.4
  1216.7 12.9 all-reduce.2
  1231.9 46.6 %all-reduce.7.cloned.1.call-done = (bf16[1,128,1536]{2,1,0:T(8,128)(2,1)}, bf16[1,128,512]{2,1,0:T(8,128)(2,1)}, bf16[1,128,2048]{2,1,0:T(8,128)(2,1)}, bf16[1,512,512]{2,1,0:T(8,128)(2,1)}) async-done(((bf16[1,128,1536]{2,1,0:T(8,128)(2,1)}, bf16[1,128,512]{2,1,0:T(8,128)(2,1)}, bf16[1,128,2048]{2,1,0:T(8,128)(2,1)}, bf16[1,512,512]{2,1,0:T(8,128)(2,1)}), (bf16[1,128,1536]{2,1,0:T(8,128)(2,1)}, ...) | async-done | bytes 1572880 | tf_op jit(solution)/shard_map/psum | solution.py:381
  (1181 shorter events, 934.9 us)
Async XLA Ops:
  7.2 66.3 %all-gather.12.cloned.1.call-start = ((), (), s32[]{:S(2)}) async-start(), calls=%async_computation.10 | async-start | bytes 1966080 | tf_op jit(solution)/shard_map/all_gather | solution.py:304
  7.9 96.7 %all-gather.16.cloned.1.call-start = ((), (), s32[]{:S(2)}) async-start(), calls=%async_computation.12 | async-start | bytes 2621440 | tf_op jit(solution)/shard_map/all_gather | solution.py:307
  8.7 96.0 %all-gather.14.cloned.1.call-start = ((), (), s32[]{:S(2)}) async-start(), calls=%async_computation.11 | async-start | bytes 2621440 | tf_op jit(solution)/shard_map/all_gather | solution.py:306
  9.4 1155.6 %reduce-scatter.13.cloned.1.call-start = ((), (), s32[]{:S(2)}) async-start(), calls=%async_computation.7 | async-start | bytes 655360 | tf_op jit(solution)/shard_map/reduce_scatter | solution.py:358
  15.9 265.0 %copy-start.180 = (f32[1,1,512]{2,1,0:T(1,128)}, f32[1,1,512]{2,1,0:T(1,128)S(1)}, u32[]{:S(2)}) copy-start(f32[1,1,512]{2,1,0:T(1,128)S(1)} %get-tuple-element.197) | copy-start | bytes 6148
  15.9 265.0 %copy-start.182 = (f32[1,1,512]{2,1,0:T(1,128)}, f32[1,1,512]{2,1,0:T(1,128)S(1)}, u32[]{:S(2)}) copy-start(f32[1,1,512]{2,1,0:T(1,128)S(1)} %get-tuple-element.198) | copy-start | bytes 6148
  15.9 289.9 %copy-start.191 = (f32[1,1,512]{2,1,0:T(1,128)}, f32[1,1,512]{2,1,0:T(1,128)S(1)}, u32[]{:S(2)}) copy-start(f32[1,1,512]{2,1,0:T(1,128)S(1)} %get-tuple-element.194) | copy-start | bytes 6148
  15.9 289.9 %copy-start.221 = (f32[1,1,512]{2,1,0:T(1,128)}, f32[1,1,512]{2,1,0:T(1,128)S(1)}, u32[]{:S(2)}) copy-start(f32[1,1,512]{2,1,0:T(1,128)S(1)} %get-tuple-element.195) | copy-start | bytes 6148
  15.9 689.0 %copy-start.158 = (f32[1,1,512]{2,1,0:T(1,128)}, f32[1,1,512]{2,1,0:T(1,128)S(1)}, u32[]{:S(2)}) copy-start(f32[1,1,512]{2,1,0:T(1,128)S(1)} %get-tuple-element.196) | copy-start | bytes 6148
  46.0 259.8 %copy-start.177 = (f32[1,1,512]{2,1,0:T(1,128)}, f32[1,1,512]{2,1,0:T(1,128)S(1)}, u32[]{:S(2)}) copy-start(f32[1,1,512]{2,1,0:T(1,128)S(1)} %get-tuple-element.210) | copy-start | bytes 6148
  73.5 232.3 %copy-start.193 = (f32[1,2048]{1,0:T(1,128)}, f32[1,2048]{1,0:T(1,128)S(1)}, u32[]{:S(2)}) copy-start(f32[1,2048]{1,0:T(1,128)S(1)} %convert_element_type.889) | copy-start | bytes 24580
  128.4 12.7 collective-permute-start
  192.4 12.9 collective-permute-start.1
  256.4 12.0 collective-permute-start.2
  319.6 12.5 collective-permute-start.3
  351.4 89.9 %copy-start.173 = (f32[392]{0:T(512)}, f32[392]{0:T(512)S(1)}, u32[]{:S(2)}) copy-start(f32[392]{0:T(512)S(1)} %div.360) | copy-start | bytes 4708
  355.7 83.8 %copy-start.161 = (f32[392]{0:T(512)}, f32[392]{0:T(512)S(1)}, u32[]{:S(2)}) copy-start(f32[392]{0:T(512)S(1)} %div.349) | copy-start | bytes 4708
  367.0 70.8 %copy-start.165 = (f32[392]{0:T(512)}, f32[392]{0:T(512)S(1)}, u32[]{:S(2)}) copy-start(f32[392]{0:T(512)S(1)} %div.338) | copy-start | bytes 4708
  373.5 62.6 %copy-start.169 = (f32[392]{0:T(512)}, f32[392]{0:T(512)S(1)}, u32[]{:S(2)}) copy-start(f32[392]{0:T(512)S(1)} %div.327) | copy-start | bytes 4708
  407.9 31.6 %copy-start.163 = (f32[392]{0:T(512)}, f32[392]{0:T(512)S(1)}, u32[]{:S(2)}) copy-start(f32[392]{0:T(512)S(1)} %rsqrt.215) | copy-start | bytes 4708
  416.1 21.7 %copy-start.167 = (f32[392]{0:T(512)}, f32[392]{0:T(512)S(1)}, u32[]{:S(2)}) copy-start(f32[392]{0:T(512)S(1)} %rsqrt.212) | copy-start | bytes 4708
  662.8 64.1 %collective-permute-start.4 = (bf16[2,14,14,512]{3,0,2,1:T(2,128)(2,1)}, bf16[2,14,14,512]{3,0,2,1:T(2,128)(2,1)}, u32[]{:S(2)}, u32[]{:S(2)}) collective-permute-start(bf16[2,14,14,512]{3,0,2,1:T(2,128)(2,1)} %get-tuple-element.114), channel_id=1, source_target_pairs={{16,0},{17,1},{18,2},{19,3},{20,4},{21,5},{22,6},{23,7},{24,8},{25... | collective-permute-start | bytes 1204232 | tf_op jit(solution)/shard_map/ppermute | solution.py:21
  784.9 11.2 collective-permute-start.5
  852.6 9.7 collective-permute-start.6
  918.2 9.7 collective-permute-start.7
  972.3 192.7 %reduce-scatter.11.cloned.1.call-start = ((), (), s32[]{:S(2)}) async-start(), calls=%async_computation.6 | async-start | bytes 1966080 | tf_op jit(solution)/shard_map/reduce_scatter | solution.py:355
  984.9 180.1 %reduce-scatter.15.cloned.1.call-start = ((), (), s32[]{:S(2)}) async-start(), calls=%async_computation.8 | async-start | bytes 2621440 | tf_op jit(solution)/shard_map/reduce_scatter | solution.py:361
  997.0 168.1 %reduce-scatter.17.cloned.1.call-start = ((), (), s32[]{:S(2)}) async-start(), calls=%async_computation.9 | async-start | bytes 2621440 | tf_op jit(solution)/shard_map/reduce_scatter | solution.py:364
  1075.0 140.1 %reduce-scatter.19.cloned.1.call-start = ((), (), s32[]{:S(2)}) async-start(), calls=%async_computation.13 | async-start | bytes 163840
  1164.0 51.9 %reduce-scatter.21.cloned.1.call-start = ((), (), s32[]{:S(2)}) async-start(), calls=%async_computation.14 | async-start | bytes 163840
  1164.9 113.6 %all-reduce.7.cloned.1.call-start = ((), (), s32[]{:S(2)}) async-start(), calls=%async_computation.15 | async-start | bytes 3145728 | tf_op jit(solution)/shard_map/psum | solution.py:381
  1190.6 20.5 %copy-start.125 = (f32[2,2,7,2,7,512]{5,0,4,3,2,1:T(2,128)S(1)}, f32[2,2,7,2,7,512]{5,0,4,3,2,1:T(2,128)}, u32[]{:S(2)}) copy-start(f32[2,2,7,2,7,512]{5,0,4,3,2,1:T(2,128)} %copy.1044) | copy-start | bytes 2408452
  (248 other events, 1270.6 us)
Sparse Core Ops, SparseCore 0:
  9.6 22.4 all-gather.11
  33.6 23.9 all-gather.15
  59.2 22.3 all-gather.13
  972.4 20.7 reduce-scatter.12
  995.6 28.0 reduce-scatter.10
  1026.1 31.1 reduce-scatter.14
  1075.1 31.0 reduce-scatter.16
  1164.1 19.4 reduce-scatter.18
  1186.6 19.7 reduce-scatter.20
  1208.8 69.6 all-reduce.6
where the time goes:
time: 1310 us; the launch traced here: 1290 us
  local copies, waits for them, and re-layouts  503 us (38%)
  matrix products  377 us (29%)
  other arithmetic  239 us (18%)
  waiting for transfers between devices  73.6 us (6%)
  blocking collectives  56.6 us (4%)
  starting transfers between devices  24.5 us (2%)
  between operations  19.3 us (1%)
    reshape x10, local copies, waits for them, and re-layouts, backward(): jnp.sum(grad_scores, axis=0)  93.8 us
    dot_general x10, matrix products, forward(): jnp.einsum('sihd,sjhd->shij', query_blocks, key_blocks, preferred_element...  49.7 us
    dot_general x20, matrix products, outer_cols(): lax.dot_general(left, right, (((1,), (1,)), ((), ())), preferred_element_...  49.6 us
    dot_general x20, matrix products, inner_rows(): lax.dot_general(left, right, (((0,), (0,)), ((), ())), preferred_element_...  47 us
    psum x1, waiting for transfers between devices, shards(): lax.psum(parted[0].astype(jnp.bfloat16), 'replica').astype(jnp.float32)  46.6 us
    dynamic_update_slice x15, other arithmetic, keep_slot(): lax.dynamic_update_index_in_dim(store, jnp.where(valid, fresh, former), p...  46.5 us
    unnamed x544, local copies, waits for them, and re-layouts  46.2 us
    dot_general x5, matrix products, backward(): jnp.einsum('hwivj,wv->ijh', summed, eye_f, precision=lax.Precision.HIGHEST)  40.3 us
  transfers between devices with their start and end apart: 18, of which 7 were waited for; matrix products, arithmetic and copies ran while one was open for 29% of the time, Pallas kernels for 0%

commit v1 on v0

--- a/solution.py
+++ b/solution.py
@@ -378,7 +378,9 @@
         ).astype(jnp.float32),
     )
     shares = (
-        lax.psum(parted[0].astype(jnp.bfloat16), "replica").astype(jnp.float32),
+        jnp.sum(lax.all_gather(parted[0].astype(jnp.bfloat16), "replica"), axis=0).astype(
+            jnp.float32
+        ),
         lax.psum(parted[1].astype(jnp.bfloat16), "replica").astype(jnp.float32),
         lax.psum(parted[2].astype(jnp.bfloat16), "replica").astype(jnp.float32),
         lax.psum(parted[3].astype(jnp.bfloat16), "replica").astype(jnp.float32),

time: 1310 us -> 1230 us (0.939)
  local copies, waits for them, and re-layouts: 503 us -> 463 us
  waiting for transfers between devices: 73.6 us -> 38.2 us
    psum x1, waiting for transfers between devices: 46.6 us -> 0.01 us  [shards(): lax.psum(parted[1].astype(jnp.bfloat16), 'replica').astype(jnp.float32)]
    unnamed x544 -> x534, local copies, waits for them, and re-layouts: 46.2 us -> 40.4 us
  transfers between devices with their start and end apart: 18 -> 19, of which waited for: 7 -> 7; matrix products, arithmetic and copies ran while one was open for 29% -> 33% of each run, Pallas kernels for 0% -> 0%
where the time goes in v1:
time: 1230 us; the launch traced here: 1210 us
  local copies, waits for them, and re-layouts  463 us (38%)
  matrix products  380 us (31%)
  other arithmetic  229 us (19%)
  blocking collectives  57.1 us (5%)
  waiting for transfers between devices  38.2 us (3%)
  starting transfers between devices  25.3 us (2%)
  between operations  19 us (2%)
    reshape x10, local copies, waits for them, and re-layouts, backward(): jnp.sum(grad_scores, axis=0)  96.8 us
    dot_general x20, matrix products, inner_rows(): lax.dot_general(left, right, (((0,), (0,)), ((), ())), preferred_element_...  52.6 us
    dot_general x20, matrix products, outer_cols(): lax.dot_general(left, right, (((1,), (1,)), ((), ())), preferred_element_...  50.2 us
    dot_general x10, matrix products, forward(): jnp.einsum('sihd,sjhd->shij', query_blocks, key_blocks, preferred_element...  49.3 us
    dot_general x5, matrix products, backward(): jnp.einsum('hwivj,wv->ijh', summed, eye_f, precision=lax.Precision.HIGHEST)  41.1 us
    unnamed x534, local copies, waits for them, and re-layouts  40.4 us
    concatenate x27, other arithmetic, to_windows(): rolled = jnp.roll(image_rows, (-offset, -offset), axis=(1, 2))  39 us
    reduce_sum x5, other arithmetic, backward(): jnp.sum(grad_scores, axis=0)  38.7 us
  transfers between devices with their start and end apart: 19, of which 7 were waited for; matrix products, arithmetic and copies ran while one was open for 33% of the time, Pallas kernels for 0%

profile of v1, /device:TPU:0, one launch (start us, length us, event | category | flops | bytes accessed | tf_op | source)
XLA Modules:
  0.0 1210.7 jit_solution(7831049563226637986)
XLA Ops:
  47.9 10.9 all-gather.4
  511.3 16.5 %fusion.14 = (f32[2,16,196]{2,1,0:T(8,128)S(1)}, f32[2,16,196]{2,1,0:T(8,128)}, f32[2,16,196]{2,1,0:T(8,128)S(1)}, f32[2,16,196]{2,1,0:T(8,128)S(1)}, f32[2,16,1...) fusion(f32[16,196,196]{1,2,0:T(8,128)S(1)} %copy.870, ...), kind=kOutput, calls=%fused_computation.39 | convolution fusion | flops 100765952 | bytes 32953872 | tf_op jit(solution)/shard_map/sihd,sjhd->shij/dot_general | solution.py:135
  527.8 19.7 %fusion.13 = (f32[2,16,196,196]{2,3,1,0:T(8,128)}, f32[2,16,196,196]{2,3,1,0:T(8,128)S(1)}, f32[2,16,196,196]{2,3,1,0:T(8,128)}, f32[2,16,196,196]{2,3,1,0:T(8,128)}, f32[2,16,196,196]{2,3,1,0:T(8,128)}) fusion(f32[2,16,196,196]{2,3,1,0:T(8,128)} %get-tuple-element.237, f32[2,16,196]{2,1,0:T(8,128)S(1)} %get-tuple-element.42, f32[16,196,196]{1,2,0:T(8,128)S(1)} %copy.870, ...), kind=kLoop, calls=%fused_computation.38 | loop fusion | flops 18439680 | bytes 51794960 | tf_op jit(solution)/shard_map/div | solution.py:139
  574.8 7.1 multiply_reduce_fusion.4
  581.9 8.2 fusion.41
  692.6 7.0 multiply_reduce_fusion.3
  699.5 7.6 fusion.43
  760.6 7.0 multiply_reduce_fusion.2
  767.6 7.6 fusion.45
  825.1 7.0 multiply_reduce_fusion.1
  832.1 7.6 fusion.47
  867.8 6.5 collective-permute-done.7
  891.1 7.4 add_convert_fusion.1
  904.5 6.5 reshape.1274
  910.9 13.1 %copy.1077 = f32[16,4,49,4,49]{4,3,1,2,0:T(4,128)} copy(f32[16,4,49,4,49]{2,1,4,3,0:T(4,128)} %reshape.1274) | data formatting | bytes 4917248 | tf_op jit(solution)/shard_map/reshape | solution.py:215
  924.1 8.1 fusion.661
  958.9 7.0 multiply_reduce_fusion
  965.9 7.7 fusion.49
  1008.1 12.8 %copy.1079 = f32[16,4,49,4,49]{4,3,1,2,0:T(4,128)} copy(f32[16,4,49,4,49]{2,1,4,3,0:T(4,128)} %reshape.1275) | data formatting | bytes 4917248 | tf_op jit(solution)/shard_map/reshape | solution.py:215
  1020.9 8.0 fusion.662
  1037.4 6.5 reshape.1276
  1043.9 12.9 %copy.1081 = f32[16,4,49,4,49]{4,3,1,2,0:T(4,128)} copy(f32[16,4,49,4,49]{2,1,4,3,0:T(4,128)} %reshape.1276) | data formatting | bytes 4917248 | tf_op jit(solution)/shard_map/reshape | solution.py:215
  1064.2 9.0 fusion.663
  1080.8 6.5 reshape.1277
  1087.2 12.7 %copy.1083 = f32[16,4,49,4,49]{4,3,1,2,0:T(4,128)} copy(f32[16,4,49,4,49]{2,1,4,3,0:T(4,128)} %reshape.1277) | data formatting | bytes 4917248 | tf_op jit(solution)/shard_map/reshape | solution.py:215
  1100.0 8.0 fusion.664
  1122.2 6.5 reshape.1278
  1128.7 13.0 %copy.1085 = f32[16,4,49,4,49]{4,3,1,2,0:T(4,128)} copy(f32[16,4,49,4,49]{2,1,4,3,0:T(4,128)} %reshape.1278) | data formatting | bytes 4917248 | tf_op jit(solution)/shard_map/reshape | solution.py:215
  1141.7 8.1 fusion.665
  1155.2 10.5 all-reduce.4
  1171.5 12.7 %all-reduce.2 = (bf16[1,6,128]{2,1,0:T(8,128)(2,1)S(1)}, bf16[1,2,128]{2,1,0:T(2,128)(2,1)S(1)}, bf16[1,512]{1,0:T(2,128)(2,1)S(1)}, bf16[1,169,4]{1,2,0:T(4,128)(2,1)S(1)}) all-reduce(bf16[1,6,128]{2,1,0:T(8,128)(2,1)S(1)} %bitcast.1055, ...), channel_id=1, replica_groups=mesh['section'=2,'fsdp'=4,'replica'=4] {'replica'}, use_global_device_ids=true, to_apply=%region_126.129 | all-reduce | flops 2212 | bytes 8848 | tf_op jit(solution)/shard_map/psum | solution.py:388
  1192.4 9.0 all-gather.20.cloned.1.call-done
  (1175 shorter events, 893.3 us)
Async XLA Ops:
  7.2 66.5 %all-gather.14.cloned.1.call-start = ((), (), s32[]{:S(2)}) async-start(), calls=%async_computation.10 | async-start | bytes 1966080 | tf_op jit(solution)/shard_map/all_gather | solution.py:304
  7.9 96.9 %all-gather.18.cloned.1.call-start = ((), (), s32[]{:S(2)}) async-start(), calls=%async_computation.12 | async-start | bytes 2621440 | tf_op jit(solution)/shard_map/all_gather | solution.py:307
  8.7 96.2 %all-gather.16.cloned.1.call-start = ((), (), s32[]{:S(2)}) async-start(), calls=%async_computation.11 | async-start | bytes 2621440 | tf_op jit(solution)/shard_map/all_gather | solution.py:306
  9.4 1063.7 %reduce-scatter.13.cloned.1.call-start = ((), (), s32[]{:S(2)}) async-start(), calls=%async_computation.7 | async-start | bytes 655360 | tf_op jit(solution)/shard_map/reduce_scatter | solution.py:358
  15.9 256.0 %copy-start.191 = (f32[1,1,512]{2,1,0:T(1,128)}, f32[1,1,512]{2,1,0:T(1,128)S(1)}, u32[]{:S(2)}) copy-start(f32[1,1,512]{2,1,0:T(1,128)S(1)} %get-tuple-element.196) | copy-start | bytes 6148
  15.9 255.9 %copy-start.193 = (f32[1,1,512]{2,1,0:T(1,128)}, f32[1,1,512]{2,1,0:T(1,128)S(1)}, u32[]{:S(2)}) copy-start(f32[1,1,512]{2,1,0:T(1,128)S(1)} %get-tuple-element.197) | copy-start | bytes 6148
  15.9 280.8 %copy-start.202 = (f32[1,1,512]{2,1,0:T(1,128)}, f32[1,1,512]{2,1,0:T(1,128)S(1)}, u32[]{:S(2)}) copy-start(f32[1,1,512]{2,1,0:T(1,128)S(1)} %get-tuple-element.193) | copy-start | bytes 6148
  15.9 280.8 %copy-start.224 = (f32[1,1,512]{2,1,0:T(1,128)}, f32[1,1,512]{2,1,0:T(1,128)S(1)}, u32[]{:S(2)}) copy-start(f32[1,1,512]{2,1,0:T(1,128)S(1)} %get-tuple-element.194) | copy-start | bytes 6148
  15.9 416.2 %copy-start.158 = (f32[1,1,512]{2,1,0:T(1,128)}, f32[1,1,512]{2,1,0:T(1,128)S(1)}, u32[]{:S(2)}) copy-start(f32[1,1,512]{2,1,0:T(1,128)S(1)} %get-tuple-element.198) | copy-start | bytes 6148
  46.0 250.7 %copy-start.188 = (f32[1,1,512]{2,1,0:T(1,128)}, f32[1,1,512]{2,1,0:T(1,128)S(1)}, u32[]{:S(2)}) copy-start(f32[1,1,512]{2,1,0:T(1,128)S(1)} %get-tuple-element.209) | copy-start | bytes 6148
  73.7 223.1 %copy-start.204 = (f32[1,2048]{1,0:T(1,128)}, f32[1,2048]{1,0:T(1,128)S(1)}, u32[]{:S(2)}) copy-start(f32[1,2048]{1,0:T(1,128)S(1)} %convert_element_type.906) | copy-start | bytes 24580
  119.3 12.7 %collective-permute-start = (bf16[2,14,14,512]{3,0,2,1:T(2,128)(2,1)}, bf16[2,14,14,512]{3,0,2,1:T(2,128)(2,1)}, u32[]{:S(2)}, u32[]{:S(2)}) collective-permute-start(bf16[2,14,14,512]{3,0,2,1:T(2,128)(2,1)} %get-tuple-element.130), channel_id=1, source_target_pairs={{0,16},{1,17},{2,18},{3,19},{4,20},{5,21},{6,22},{7,23},{8,24},{9,... | collective-permute-start | bytes 1204232 | tf_op jit(solution)/shard_map/ppermute | solution.py:21
  183.3 12.9 %collective-permute-start.1 = (bf16[2,14,14,512]{3,0,2,1:T(2,128)(2,1)}, bf16[2,14,14,512]{3,0,2,1:T(2,128)(2,1)}, u32[]{:S(2)}, u32[]{:S(2)}) collective-permute-start(bf16[2,14,14,512]{3,0,2,1:T(2,128)(2,1)} %get-tuple-element.128), channel_id=1, source_target_pairs={{0,16},{1,17},{2,18},{3,19},{4,20},{5,21},{6,22},{7,23},{8,24},{9,... | collective-permute-start | bytes 1204232 | tf_op jit(solution)/shard_map/ppermute | solution.py:21
  247.3 12.1 collective-permute-start.2
  310.6 12.5 %collective-permute-start.3 = (bf16[2,14,14,512]{3,0,2,1:T(2,128)(2,1)S(1)}, bf16[2,14,14,512]{3,0,2,1:T(2,128)(2,1)S(1)}, u32[]{:S(2)}, u32[]{:S(2)}) collective-permute-start(bf16[2,14,14,512]{3,0,2,1:T(2,128)(2,1)S(1)} %get-tuple-element.124), channel_id=1, source_target_pairs={{0,16},{1,17},{2,18},{3,19},{4,20},{5,21},{6,22},{7,23},{8,24},{9,... | collective-permute-start | bytes 1204232 | tf_op jit(solution)/shard_map/ppermute | solution.py:21
  342.2 89.9 %copy-start.184 = (f32[392]{0:T(512)}, f32[392]{0:T(512)S(1)}, u32[]{:S(2)}) copy-start(f32[392]{0:T(512)S(1)} %div.360) | copy-start | bytes 4708
  346.6 83.8 %copy-start.168 = (f32[392]{0:T(512)}, f32[392]{0:T(512)S(1)}, u32[]{:S(2)}) copy-start(f32[392]{0:T(512)S(1)} %div.349) | copy-start | bytes 4708
  357.9 70.8 %copy-start.170 = (f32[392]{0:T(512)}, f32[392]{0:T(512)S(1)}, u32[]{:S(2)}) copy-start(f32[392]{0:T(512)S(1)} %div.338) | copy-start | bytes 4708
  364.3 62.7 %copy-start.172 = (f32[392]{0:T(512)}, f32[392]{0:T(512)S(1)}, u32[]{:S(2)}) copy-start(f32[392]{0:T(512)S(1)} %div.327) | copy-start | bytes 4708
  374.9 250.8 %copy-start.176 = (f32[392]{0:T(512)}, f32[392]{0:T(512)S(1)}, u32[]{:S(2)}) copy-start(f32[392]{0:T(512)S(1)} %div.316) | copy-start | bytes 4708
  423.5 202.2 %copy-start.182 = (f32[392]{0:T(512)}, f32[392]{0:T(512)S(1)}, u32[]{:S(2)}) copy-start(f32[392]{0:T(512)S(1)} %rsqrt.206) | copy-start | bytes 4708
  635.6 40.6 %collective-permute-start.4 = (bf16[2,14,14,512]{3,0,2,1:T(2,128)(2,1)}, bf16[2,14,14,512]{3,0,2,1:T(2,128)(2,1)}, u32[]{:S(2)}, u32[]{:S(2)}) collective-permute-start(bf16[2,14,14,512]{3,0,2,1:T(2,128)(2,1)} %get-tuple-element.113), channel_id=1, source_target_pairs={{16,0},{17,1},{18,2},{19,3},{20,4},{21,5},{22,6},{23,7},{24,8},{25... | collective-permute-start | bytes 1204232 | tf_op jit(solution)/shard_map/ppermute | solution.py:21
  733.2 11.2 collective-permute-start.5
  800.0 9.7 collective-permute-start.6
  864.5 9.9 collective-permute-start.7
  887.9 185.3 %reduce-scatter.15.cloned.1.call-start = ((), (), s32[]{:S(2)}) async-start(), calls=%async_computation.8 | async-start | bytes 2621440 | tf_op jit(solution)/shard_map/reduce_scatter | solution.py:361
  898.5 174.7 %reduce-scatter.17.cloned.1.call-start = ((), (), s32[]{:S(2)}) async-start(), calls=%async_computation.9 | async-start | bytes 2621440 | tf_op jit(solution)/shard_map/reduce_scatter | solution.py:364
  949.2 162.7 %reduce-scatter.11.cloned.1.call-start = ((), (), s32[]{:S(2)}) async-start(), calls=%async_computation.6 | async-start | bytes 1966080 | tf_op jit(solution)/shard_map/reduce_scatter | solution.py:355
  994.1 175.7 %reduce-scatter.19.cloned.1.call-start = ((), (), s32[]{:S(2)}) async-start(), calls=%async_computation.14 | async-start | bytes 163840
  1062.8 107.8 %reduce-scatter.21.cloned.1.call-start = ((), (), s32[]{:S(2)}) async-start(), calls=%async_computation.15 | async-start | bytes 163840
  1063.7 122.8 %all-reduce.7.cloned.1.call-start = ((), (), s32[]{:S(2)}) async-start(), calls=%async_computation.16 | async-start | bytes 2359296 | tf_op jit(solution)/shard_map/psum | solution.py:384
  1073.2 128.2 %all-gather.20.cloned.1.call-start = ((), (), s32[]{:S(2)}) async-start(), calls=%async_computation.13 | async-start | bytes 1966080 | tf_op jit(solution)/shard_map/all_gather | solution.py:381
  (244 other events, 1284.3 us)
Sparse Core Ops, SparseCore 0:
  9.6 22.4 all-gather.13
  33.6 24.0 all-gather.17
  59.2 22.3 all-gather.15
  888.0 20.8 reduce-scatter.12
  911.2 31.1 reduce-scatter.14
  949.3 30.2 reduce-scatter.16
  994.2 27.1 reduce-scatter.10
  1062.9 19.2 reduce-scatter.18
  1084.6 19.6 reduce-scatter.20
  1106.7 56.0 all-reduce.6
  1164.4 36.9 all-gather.19
